TPU v7x, 32 devices: a whole 2x2x4 slice. The times are simulated.
32 devices in a mesh: groups: 2 (over y), seq: 4 (over z), dp: 2 (over x), mp: 2 (over core).
Axes of the slice: x: 2, y: 2, z: 4, core: 2. Of those that a mesh axis runs over, the one named last changes fastest.
Arguments:
- tiles: bfloat16 [160, 8, 8, 768], P(('groups', 'seq', 'dp')), parts along dimension 0, may hold values from -6 to 6
- token_grad: bfloat16 [160, 8, 8, 768], P(('groups', 'seq', 'dp')), parts along dimension 0, may hold values from -1.5 to 1.5
- embed_grad: bfloat16 [2, 80, 768], P('dp', 'groups', 'seq'), parts along dimension 1, may hold values from -48 to 48
- live_tiles: int32 [16], P(('groups', 'seq', 'dp')), parts along dimension 0, may hold values from 1 to 10, 60 in all
- dw_kernel: float32 [7, 7, 768], replicated, may hold values from -0.875 to 0.875
- dw_bias: float32 [768], replicated, may hold values from -3 to 3
- ln_gain: float32 [768], replicated, may hold values from 0.1 to 1.9
- ln_bias: float32 [768], replicated, may hold values from -2 to 2
- w_up: bfloat16 [768, 2560], P('seq', 'mp'), may hold values from -0.21875 to 0.21875
- b_up: float32 [2560], P('mp'), may hold values from -3 to 3
- w_down: bfloat16 [768, 2560], P('seq', 'mp'), may hold values from -0.125 to 0.125
- layer_scale: float32 [768], replicated, may hold values from 0.3 to 1.5
Outputs:
- tile_grad: bfloat16 [160, 8, 8, 768], P(('groups', 'seq', 'dp')), parts along dimension 0
- grad_up: float32 [1536, 2560], P(('groups', 'seq'), 'mp'), parts along dimension 0
- grad_down: float32 [1536, 2560], P(('groups', 'seq'), 'mp'), parts along dimension 0
There are 2 independent parts, one for each index of `groups`. A program takes and returns all parts, laid end to end along the dimension named above; an argument that names none is the same for every part. Nothing has to cross between parts.
Inputs may be any that keep to these rules, and one draw needn't show every extreme that they name: Each loader's foreground tiles fill its slots 0 to live_tiles - 1 of 10; some loader has all 10.
All inputs are finite; a program needn't handle non-finite values. No bound on the sum of `live_tiles` on one device may be relied on, other than what follows from the above.
Results may differ from a plain program's by a relative error of at most 0.01.
Values may be sent and summed in bfloat16 or wider, within the bound.
No kernel may reach another device: no remote copies, remote signals or barrier semaphores. Data moves between devices by JAX's collectives and lax.ppermute only.
A program may use at most 64 MiB of HBM per device.

v0:
```python
import jax
import jax.numpy as jnp
from jax import lax
from jax.sharding import PartitionSpec as P

sqrt_two_pi = 0.7978845608028654
cubic_coef = 0.044715


def depthwise(values, kernel):
    reach = kernel.shape[0]
    margin = reach // 2
    height = values.shape[1]
    padded = jnp.pad(values, ((0, 0), (margin, margin), (margin, margin), (0, 0)))
    total = jnp.zeros(values.shape, jnp.float32)
    for row_off in range(reach):
        for col_off in range(reach):
            total = (
                total
                + padded[:, row_off : row_off + height, col_off : col_off + height, :]
                * kernel[row_off, col_off]
            )
    return total


def gelu_tanh(values):
    inner = sqrt_two_pi * (values + cubic_coef * values * values * values)
    return 0.5 * values * (1.0 + jnp.tanh(inner))


def gelu_slope(values):
    tangent = jnp.tanh(sqrt_two_pi * (values + cubic_coef * values * values * values))
    return 0.5 * (1.0 + tangent) + 0.5 * values * (1.0 - tangent * tangent) * sqrt_two_pi * (
        1.0 + 3.0 * cubic_coef * values * values
    )


def normalize(values):
    center = jnp.mean(values, axis=-1, keepdims=True)
    shifted = values - center
    spread = jnp.sqrt(jnp.mean(shifted * shifted, axis=-1, keepdims=True) + 1e-06)
    return (shifted / spread, spread)


def norm_backward(normed_grad, normal, spread, ln_gain):
    scaled = normed_grad * ln_gain
    return (
        scaled
        - jnp.mean(scaled, axis=-1, keepdims=True)
        - normal * jnp.mean(scaled * normal, axis=-1, keepdims=True)
    ) / spread


def on_device(
    tiles,
    token_grad,
    embed_grad,
    live_tiles,
    dw_kernel,
    dw_bias,
    ln_gain,
    ln_bias,
    w_up,
    b_up,
    w_down,
    layer_scale,
):
    count = tiles.shape[0]
    height = tiles.shape[1]
    width = tiles.shape[3]
    flipped = dw_kernel[::-1, ::-1, :]
    arrived = lax.all_to_all(embed_grad[0], "seq", split_axis=0, concat_axis=1, tiled=True)
    live = (jnp.arange(count) < live_tiles[0]).astype(jnp.float32)[:, None, None, None]
    pooled = arrived.astype(jnp.float32)[:, None, None, :] * live
    out_grad = live * token_grad.astype(jnp.float32) + pooled / (height * height)
    branch_grad = (layer_scale * out_grad).astype(jnp.bfloat16).reshape(-1, width)
    conv = depthwise(tiles.astype(jnp.float32), dw_kernel) + dw_bias
    normal, spread = normalize(conv)
    normed = (normal * ln_gain + ln_bias).astype(jnp.bfloat16)
    rows = normed.reshape(-1, width)
    full_up, full_down = (
        lax.all_gather(w_up, "seq", axis=0, tiled=True),
        lax.all_gather(w_down, "seq", axis=0, tiled=True),
    )
    hidden = jnp.dot(rows, full_up, preferred_element_type=jnp.float32) + b_up
    act = gelu_tanh(hidden).astype(jnp.bfloat16)
    act_grad = jnp.dot(branch_grad, full_down, preferred_element_type=jnp.float32)
    hidden_grad = (act_grad * gelu_slope(hidden)).astype(jnp.bfloat16)
    normed_part = lax.dot_general(
        hidden_grad, full_up, (((1,), (1,)), ((), ())), preferred_element_type=jnp.float32
    )
    part_down = lax.dot_general(
        branch_grad, act, (((0,), (0,)), ((), ())), preferred_element_type=jnp.float32
    )
    part_up = lax.dot_general(
        rows, hidden_grad, (((0,), (0,)), ((), ())), preferred_element_type=jnp.float32
    )
    up_piece, down_piece = (
        lax.psum_scatter(
            part_up.astype(jnp.bfloat16), "seq", scatter_dimension=0, tiled=True
        ).astype(jnp.float32),
        lax.psum_scatter(
            part_down.astype(jnp.bfloat16), "seq", scatter_dimension=0, tiled=True
        ).astype(jnp.float32),
    )
    grad_up, grad_down = (
        lax.psum(up_piece.astype(jnp.bfloat16), "dp").astype(jnp.float32),
        lax.psum(down_piece.astype(jnp.bfloat16), "dp").astype(jnp.float32),
    )
    normed_grad = lax.psum(normed_part.astype(jnp.bfloat16), "mp").astype(jnp.float32)
    conv_grad = norm_backward(normed_grad.reshape(conv.shape), normal, spread, ln_gain)
    tile_grad = (out_grad + depthwise(conv_grad, flipped)).astype(jnp.bfloat16)
    return (tile_grad, grad_up, grad_down)


def solution(mesh):
    return jax.shard_map(
        on_device,
        mesh=mesh,
        in_specs=(
            P(("groups", "seq", "dp"), None, None, None),
            P(("groups", "seq", "dp"), None, None, None),
            P("dp", "groups", "seq"),
            P(("groups", "seq", "dp")),
            P(),
            P(),
            P(),
            P(),
            P("seq", "mp"),
            P("mp"),
            P("seq", "mp"),
            P(),
        ),
        out_specs=(
            P(("groups", "seq", "dp"), None, None, None),
            P(("groups", "seq"), "mp"),
            P(("groups", "seq"), "mp"),
        ),
        check_vma=False,
    )
```

profile of v0, /device:TPU:0, one launch (start us, length us, event | category | flops | bytes accessed | tf_op | source)
XLA Modules:
  0.0 267.0 jit_solution(10190657379910288535)
XLA Ops:
  7.2 0.7 all-gather.5.cloned.1.call-update
  7.9 0.7 all_to_all.10
  8.7 0.7 reshape.223
  9.4 6.5 %all-to-all-start = ((bf16[4,2,960]{2,1,0:T(2,128)(2,1)}), bf16[4,2,960]{2,1,0:T(2,128)(2,1)S(1)}, u32[]{:S(2)}, u32[]{:S(2)}) async-start(bf16[4,2,960]{2,1,0:T(2,128)(2,1)} %reshape.223), calls=%async_computation | async-start | bytes 32768 | tf_op jit(solution)/shard_map/all_to_all | solution.py:72
  15.8 0.7 all-gather.3.cloned.1.call-update
  16.6 1.1 slice_reduce_fusion.46
  17.7 1.4 slice_reduce_fusion.48
  19.1 1.4 slice_reduce_fusion.47
  20.5 0.2 convert_element_type.70
  20.7 13.0 %fusion.209 = (f32[10,8,8]{2,1,0:T(8,128)S(1)}, f32[10,8,8,768]{3,2,1,0:T(8,128)S(1)}) fusion(f32[768]{0:T(1024)S(1)} %copy-done.5, f32[768]{0:T(1024)S(1)} %get-tuple-element.50, f32[768]{0:T(1024)S(1)} %get-tuple-element.51, f32[768]{0:T(1024)S(1)} %get-tuple-element.4, f32[768]{0:T(1024)S(1)} %get-tuple-element.5, f32[768]{0:T(1024)S(1)} %get-tuple-element.6, ...), kind=kLoop, calls=%fused_computation.377 | loop fusion | flops 48659840 | bytes 4088320 | tf_op jit(solution)/shard_map/reduce_sum | solution.py:39
  34.4 0.3 multiply_reduce_fusion.2
  34.8 1.3 add_convert_fusion
  36.4 1.3 multiply_convert_fusion.1
  37.7 18.1 %all-gather.5.cloned.1.call-done = bf16[768,1280]{1,0:T(8,128)(2,1)} async-done(((bf16[192,1280]{1,0:T(8,128)(2,1)}), bf16[768,1280]{1,0:T(8,128)(2,1)}) %all-gather.5.cloned.1.call-update) | async-done | bytes 1966096 | tf_op jit(solution)/shard_map/all_gather | solution.py:82
  55.9 5.0 %convolution_add_fusion = f32[640,1280]{1,0:T(8,128)} fusion(bf16[640,768]{1,0:T(8,128)(2,1)} %bitcast.18, bf16[768,1280]{1,0:T(8,128)(2,1)} %all-gather.5.cloned.1.call-done, f32[1280]{0:T(1024)S(1)} %copy-done.7), kind=kOutput, calls=%fused_computation.99 | convolution fusion | flops 1259110400 | bytes 6231040 | tf_op jit(solution)/shard_map/dot_general | solution.py:85
  60.9 39.0 %all-gather.3.cloned.1.call-done = bf16[768,1280]{1,0:T(8,128)(2,1)} async-done(((bf16[192,1280]{1,0:T(8,128)(2,1)}), bf16[768,1280]{1,0:T(8,128)(2,1)}) %all-gather.3.cloned.1.call-update) | async-done | bytes 1966096 | tf_op jit(solution)/shard_map/all_gather | solution.py:83
  99.9 5.7 %fusion.5 = bf16[640,1280]{1,0:T(8,128)(2,1)S(1)} fusion(f32[640,1280]{1,0:T(8,128)} %convolution_add_fusion, bf16[640,768]{1,0:T(8,128)(2,1)} %bitcast.20, bf16[768,1280]{1,0:T(8,128)(2,1)} %all-gather.3.cloned.1.call-done), kind=kOutput, calls=%fused_computation.108 | convolution fusion | flops 1273856000 | bytes 7864320 | tf_op jit(solution)/shard_map/dot_general | solution.py:87
  105.6 1.2 copy-done.8
  106.8 2.4 convolution_convert_fusion.2
  109.3 4.8 %convolution_convert_fusion.1 = bf16[768,1280]{1,0:T(8,128)(2,1)} fusion(bf16[640,768]{1,0:T(8,128)(2,1)} %bitcast.19, bf16[640,1280]{1,0:T(8,128)(2,1)} %copy-done.8), kind=kOutput, calls=%fused_computation.101 | convolution fusion | flops 1259274240 | bytes 4587520 | tf_op jit(solution)/shard_map/dot_general | solution.py:95
  114.1 0.2 reduce-scatter.5.cloned.1.call-start
  114.3 5.5 %convolution_convert_fusion = bf16[768,1280]{1,0:T(8,128)(2,1)} fusion(bf16[640,768]{1,0:T(8,128)(2,1)} %bitcast.21, f32[640,1280]{1,0:T(8,128)} %convolution_add_fusion), kind=kOutput, calls=%fused_computation.100 | convolution fusion | flops 1266647040 | bytes 6225920 | tf_op jit(solution)/shard_map/dot_general | solution.py:92
  119.9 7.8 %all-reduce.6.cloned.1.call-done = bf16[640,768]{1,0:T(8,128)(2,1)} async-done(((bf16[640,768]{1,0:T(8,128)(2,1)}), bf16[640,768]{1,0:T(8,128)(2,1)}) %all-reduce.6.cloned.1.call-update) | async-done | bytes 983056 | tf_op jit(solution)/shard_map/psum | solution.py:110
  127.7 1.5 multiply_reduce_fusion.1
  129.3 1.8 multiply_reduce_fusion
  131.1 1.9 subtract_divide_fusion
  133.0 39.7 %reduce-scatter.3.cloned.1.call-done = bf16[192,1280]{1,0:T(8,128)(2,1)} async-done(((bf16[768,1280]{1,0:T(8,128)(2,1)}), bf16[192,1280]{1,0:T(8,128)(2,1)}) %reduce-scatter.3.cloned.1.call-update) | async-done | bytes 491536 | tf_op jit(solution)/shard_map/reduce_scatter | solution.py:99
  172.7 43.0 %reduce-scatter.5.cloned.1.call-done = bf16[192,1280]{1,0:T(8,128)(2,1)} async-done(((bf16[768,1280]{1,0:T(8,128)(2,1)}), bf16[192,1280]{1,0:T(8,128)(2,1)}) %reduce-scatter.5.cloned.1.call-update) | async-done | bytes 491536 | tf_op jit(solution)/shard_map/reduce_scatter | solution.py:102
  215.7 38.3 %fusion.200 = bf16[10,8,8,768]{3,2,1,0:T(8,128)(2,1)} fusion(f32[10,8,8,768]{3,2,1,0:T(8,128)} %subtract_divide_fusion, bf16[10,8,8,768]{3,2,1,0:T(8,128)(2,1)S(1)} %copy-done, f32[768]{0:T(1024)S(1)} %get-tuple-element.50, f32[768]{0:T(1024)S(1)} %get-tuple-element.51, f32[768]{0:T(1024)S(1)} %get-tuple-element.4, f32[768]{0:T(1024)S(1)} %get-tuple-element.5, ...), kind=kLoop, calls=%fused_computation.310 | loop fusion | flops 50135040 | bytes 4113448 | tf_op jit(solution)/shard_map/convert_element_type | solution.py:112
  254.0 2.1 all-reduce.8.cloned.1.call-done
  256.1 2.0 convert_element_type.77
  258.1 2.0 convert_element_type.80
  (38 shorter events, 0.7 us)
Async XLA Ops:
  7.2 13.3 %copy-start.1 = (bf16[10,8,8,768]{3,2,1,0:T(8,128)(2,1)S(1)}, bf16[10,8,8,768]{3,2,1,0:T(8,128)(2,1)}, u32[]{:S(2)}) copy-start(bf16[10,8,8,768]{3,2,1,0:T(8,128)(2,1)} %param.12) | copy-start | bytes 2949124
  7.2 48.7 %all-gather.5.cloned.1.call-start = ((), (), s32[]{:S(2)}) async-start(), calls=%async_computation.4 | async-start | bytes 2457600 | tf_op jit(solution)/shard_map/all_gather | solution.py:82
  9.4 11.3 %copy-start.5 = (f32[768]{0:T(1024)S(1)}, f32[768]{0:T(1024)}, u32[]{:S(2)}) copy-start(f32[768]{0:T(1024)} %param.17) | copy-start | bytes 9220
  9.4 26.7 %all-to-all-start = ((bf16[4,2,960]{2,1,0:T(2,128)(2,1)}), bf16[4,2,960]{2,1,0:T(2,128)(2,1)S(1)}, u32[]{:S(2)}, u32[]{:S(2)}) async-start(bf16[4,2,960]{2,1,0:T(2,128)(2,1)} %reshape.223), calls=%async_computation | async-start | bytes 32768 | tf_op jit(solution)/shard_map/all_to_all | solution.py:72
  15.8 84.0 %all-gather.3.cloned.1.call-start = ((), (), s32[]{:S(2)}) async-start(), calls=%async_computation.3 | async-start | bytes 2457600 | tf_op jit(solution)/shard_map/all_gather | solution.py:83
  16.6 111.2 %all-reduce.6.cloned.1.call-start = ((), (), s32[]{:S(2)}) async-start(), calls=%async_computation.5 | async-start | bytes 1966080 | tf_op jit(solution)/shard_map/psum | solution.py:110
  33.6 1.1 copy-start.2
  33.7 1.1 copy-start.3
  34.7 1.7 copy-start
  34.7 1.7 copy-start.4
  36.1 19.8 %copy-start.7 = (f32[1280]{0:T(1024)S(1)}, f32[1280]{0:T(1024)}, u32[]{:S(2)}) copy-start(f32[1280]{0:T(1024)} %param.21) | copy-start | bytes 15364
  99.9 6.9 %copy-start.6 = (bf16[768,1280]{1,0:T(8,128)(2,1)S(1)}, bf16[768,1280]{1,0:T(8,128)(2,1)}, u32[]{:S(2)}) copy-start(bf16[768,1280]{1,0:T(8,128)(2,1)} %all-gather.5.cloned.1.call-done) | copy-start | bytes 5898244
  105.5 1.2 copy-start.8
  109.2 63.4 %reduce-scatter.3.cloned.1.call-start = ((), (), s32[]{:S(2)}) async-start(), calls=%async_computation.6 | async-start | bytes 2457600 | tf_op jit(solution)/shard_map/reduce_scatter | solution.py:99
  114.1 101.5 %reduce-scatter.5.cloned.1.call-start = ((), (), s32[]{:S(2)}) async-start(), calls=%async_computation.7 | async-start | bytes 2457600 | tf_op jit(solution)/shard_map/reduce_scatter | solution.py:102
  119.9 136.2 %all-reduce.8.cloned.1.call-start = ((), (), s32[]{:S(2)}) async-start(), calls=%async_computation.8 | async-start | bytes 1966080 | tf_op jit(solution)/shard_map/psum | solution.py:107
Sparse Core Ops, SparseCore 0:
  9.6 46.2 all-gather.4
  57.4 42.3 all-gather.2
  109.3 18.3 all-reduce.5
  130.0 42.6 reduce-scatter.2
  174.9 40.6 reduce-scatter.4
  218.0 38.0 all-reduce.7
where the time goes:
time: 268 us; the launch traced here: 267 us
  waiting for transfers between devices  151 us (56%)
  other arithmetic  63.8 us (24%)
  matrix products  23.4 us (9%)
  between operations  14.9 us (6%)
  local copies, waits for them, and re-layouts  6.86 us (3%)
  starting transfers between devices  6.85 us (3%)
    reduce_scatter x1, waiting for transfers between devices, on_device(): lax.psum_scatter(part_down.astype(jnp.bfloat16), 'seq', scatter_dimension...  43 us
    reduce_scatter x1, waiting for transfers between devices, on_device(): lax.psum_scatter(part_up.astype(jnp.bfloat16), 'seq', scatter_dimension=0...  39.7 us
    all_gather x1, waiting for transfers between devices, on_device(): lax.all_gather(w_down, 'seq', axis=0, tiled=True)  39 us
    convert_element_type x1, other arithmetic, on_device(): tile_grad = (out_grad + depthwise(conv_grad, flipped)).astype(jnp.bfloat16)  38.3 us
    all_gather x1, waiting for transfers between devices, on_device(): lax.all_gather(w_up, 'seq', axis=0, tiled=True)  18.1 us
    reduce_sum x1, other arithmetic, normalize(): center = jnp.mean(values, axis=-1, keepdims=True)  13 us
    psum x1, waiting for transfers between devices, on_device(): lax.psum(normed_part.astype(jnp.bfloat16), 'mp').astype(jnp.float32)  7.78 us
    all_to_all x1, starting transfers between devices, on_device(): lax.all_to_all(embed_grad[0], 'seq', split_axis=0, concat_axis=1, tiled=T...  6.46 us
  transfers between devices with their start and end apart: 7, of which 6 were waited for; matrix products, arithmetic and copies ran while one was open for 30% of the time, Pallas kernels for 0%

commit v1 on v0

--- a/solution.py
+++ b/solution.py
@@ -5,6 +5,28 @@
 
 sqrt_two_pi = 0.7978845608028654
 cubic_coef = 0.044715
+
+
+def joined_along(blocks, dim):
+    shape = list(blocks.shape[1:])
+    shape[dim] *= blocks.shape[0]
+    return jnp.moveaxis(blocks, 0, dim).reshape(shape)
+
+
+def gather_around(value, axis, dim):
+    size = lax.axis_size(axis)
+    pairs = [(i, (i + 1) % size) for i in range(size)]
+    back = [(b, a) for a, b in pairs]
+    lower, upper = ([], [])
+    for hop in range(size - 1):
+        if hop % 2 == 0:
+            lower.append(lax.ppermute(lower[-1] if lower else value, axis, pairs))
+        else:
+            upper.append(lax.ppermute(upper[-1] if upper else value, axis, back))
+    pieces = jnp.stack([*lower[::-1], value, *upper])
+    shift = lax.axis_index(axis) - len(lower)
+    pieces = pieces[(jnp.arange(size) - shift) % size]
+    return joined_along(pieces, dim)
 
 
 def depthwise(values, kernel):
@@ -79,7 +101,7 @@
     normed = (normal * ln_gain + ln_bias).astype(jnp.bfloat16)
     rows = normed.reshape(-1, width)
     full_up, full_down = (
-        lax.all_gather(w_up, "seq", axis=0, tiled=True),
+        gather_around(w_up, "seq", 0),
         lax.all_gather(w_down, "seq", axis=0, tiled=True),
     )
     hidden = jnp.dot(rows, full_up, preferred_element_type=jnp.float32) + b_up

time: 268 us -> 257 us (0.959)
  waiting for transfers between devices: 151 us -> 120 us
  other arithmetic: 63.8 us -> 71.6 us
  local copies, waits for them, and re-layouts: 6.86 us -> 14.4 us
  starting transfers between devices: 6.85 us -> 9.8 us
    all_gather x1, waiting for transfers between devices: 39 us -> 0.01 us  [on_device(): lax.all_gather(w_down, 'seq', axis=0, tiled=True)]
    all_gather x1 -> x0, waiting for transfers between devices: 18.1 us -> none  [on_device(): lax.all_gather(w_up, 'seq', axis=0, tiled=True)]
    ppermute x0 -> x3, waiting for transfers between devices: none -> 15.1 us  [the longest x2 15.1 us: gather_around(): lower.append(lax.ppermute(lower[-1] if lower else value, axis, pairs))]
    all_to_all x1, waiting for transfers between devices: 0.01 us -> 14.6 us  [on_device(): lax.all_to_all(embed_grad[0], 'seq', split_axis=0, concat_axis=1, tiled=T...]
    ppermute x0 -> x3, starting transfers between devices: none -> 5.57 us  [the longest x2 3.47 us: gather_around(): lower.append(lax.ppermute(lower[-1] if lower else value, axis, pairs))]
    gather x0 -> x1, local copies, waits for them, and re-layouts: none -> 3.66 us  [gather_around(): pieces = pieces[(jnp.arange(size) - shift) % size]]
    reduce_scatter x1, waiting for transfers between devices: 43 us -> 39.4 us  [on_device(): lax.psum_scatter(part_down.astype(jnp.bfloat16), 'seq', scatter_dimension...]
    reduce_scatter x1, waiting for transfers between devices: 39.7 us -> 43 us  [on_device(): lax.psum_scatter(part_up.astype(jnp.bfloat16), 'seq', scatter_dimension=0...]
  transfers between devices with their start and end apart: 7 -> 9, of which waited for: 6 -> 6; matrix products, arithmetic and copies ran while one was open for 30% -> 37% of each run, Pallas kernels for 0% -> 0%
where the time goes in v1:
time: 257 us; the launch traced here: 256 us
  waiting for transfers between devices  120 us (47%)
  other arithmetic  71.6 us (28%)
  matrix products  23.5 us (9%)
  between operations  15.8 us (6%)
  local copies, waits for them, and re-layouts  14.4 us (6%)
  starting transfers between devices  9.8 us (4%)
    reduce_scatter x1, waiting for transfers between devices, on_device(): lax.psum_scatter(part_up.astype(jnp.bfloat16), 'seq', scatter_dimension=0...  43 us
    convert_element_type x1, other arithmetic, on_device(): tile_grad = (out_grad + depthwise(conv_grad, flipped)).astype(jnp.bfloat16)  39.8 us
    reduce_scatter x1, waiting for transfers between devices, on_device(): lax.psum_scatter(part_down.astype(jnp.bfloat16), 'seq', scatter_dimension...  39.4 us
    ppermute x2, waiting for transfers between devices, gather_around(): lower.append(lax.ppermute(lower[-1] if lower else value, axis, pairs))  15.1 us
    all_to_all x1, waiting for transfers between devices, on_device(): lax.all_to_all(embed_grad[0], 'seq', split_axis=0, concat_axis=1, tiled=T...  14.6 us
    reduce_sum x1, other arithmetic, normalize(): center = jnp.mean(values, axis=-1, keepdims=True)  12.8 us
    psum x1, waiting for transfers between devices, on_device(): lax.psum(normed_part.astype(jnp.bfloat16), 'mp').astype(jnp.float32)  8.04 us
    dot_general x1, matrix products, on_device(): jnp.dot(branch_grad, full_down, preferred_element_type=jnp.float32)  5.67 us
  transfers between devices with their start and end apart: 9, of which 6 were waited for; matrix products, arithmetic and copies ran while one was open for 37% of the time, Pallas kernels for 0%

profile of v1, /device:TPU:0, one launch (start us, length us, event | category | flops | bytes accessed | tf_op | source)
XLA Modules:
  0.0 255.6 jit_solution(2880195667865687719)
XLA Ops:
  7.2 3.1 %collective-permute-start = (bf16[192,1280]{1,0:T(8,128)(2,1)}, bf16[192,1280]{1,0:T(8,128)(2,1)}, u32[]{:S(2)}, u32[]{:S(2)}) collective-permute-start(bf16[192,1280]{1,0:T(8,128)(2,1)} %param.20), channel_id=1, source_target_pairs={{0,4},{4,8},{8,12},{12,0},{1,5},{5,9},{9,13},{13,1},{2,6},{6,10},{... | collective-permute-start | bytes 1474568 | tf_op jit(solution)/shard_map/ppermute | solution.py:23
  10.3 2.1 collective-permute-start.2
  13.9 3.8 %all-to-all-start = ((bf16[4,2,960]{2,1,0:T(2,128)(2,1)}), bf16[4,2,960]{2,1,0:T(2,128)(2,1)}, u32[]{:S(2)}, u32[]{:S(2)}) async-start(bf16[4,2,960]{2,1,0:T(2,128)(2,1)} %reshape.284), calls=%async_computation | async-start | bytes 32768 | tf_op jit(solution)/shard_map/all_to_all | solution.py:94
  17.8 1.1 slice_reduce_fusion.46
  19.0 1.4 slice_reduce_fusion.48
  20.6 2.0 slice_reduce_fusion.47
  22.6 1.4 convert_element_type.70
  24.0 12.8 %fusion.211 = (f32[10,8,8]{2,1,0:T(8,128)S(1)}, f32[10,8,8,768]{3,2,1,0:T(8,128)S(1)}) fusion(f32[768]{0:T(1024)S(1)} %copy-done.86, f32[768]{0:T(1024)S(1)} %get-tuple-element.50, f32[768]{0:T(1024)S(1)} %get-tuple-element.51, f32[768]{0:T(1024)S(1)} %get-tuple-element.4, f32[768]{0:T(1024)S(1)} %get-tuple-element.5, f32[768]{0:T(1024)S(1)} %get-tuple-element.6, ...), kind=kLoop, calls=%fused_computation.386 | loop fusion | flops 48659840 | bytes 4088320 | tf_op jit(solution)/shard_map/reduce_sum | solution.py:61
  37.9 1.3 add_convert_fusion
  41.1 14.6 %all-to-all-done = bf16[4,2,960]{2,1,0:T(2,128)(2,1)} async-done(((bf16[4,2,960]{2,1,0:T(2,128)(2,1)}), bf16[4,2,960]{2,1,0:T(2,128)(2,1)}, u32[]{:S(2)}, u32[]{:S(2)}) %all-to-all-start) | async-done | bytes 15392 | tf_op jit(solution)/shard_map/all_to_all | solution.py:94
  55.6 0.8 reshape.285
  57.1 1.5 reshape.226
  59.0 0.9 multiply_multiply_fusion.1
  59.9 2.0 multiply_convert_fusion.1
  61.9 15.1 %collective-permute-done.1 = bf16[192,1280]{1,0:T(8,128)(2,1)S(1)} collective-permute-done((bf16[192,1280]{1,0:T(8,128)(2,1)}, bf16[192,1280]{1,0:T(8,128)(2,1)S(1)}, u32[]{:S(2)}, u32[]{:S(2)}) %collective-permute-start.1) | collective-permute-done | bytes 491552 | tf_op jit(solution)/shard_map/ppermute | solution.py:23
  77.0 2.7 %pad_maximum_fusion = bf16[4,192,1280]{2,1,0:T(8,128)(2,1)} fusion(bf16[1,192,1280]{2,1,0:T(8,128)(2,1)} %bitcast.7, bf16[1,192,1280]{2,1,0:T(8,128)(2,1)S(1)} %bitcast.31, bf16[1,192,1280]{2,1,0:T(8,128)(2,1)} %bitcast.5, bf16[1,192,1280]{2,1,0:T(8,128)(2,1)S(1)} %bitcast.32), kind=kLoop, calls=%fused_computation.304 | loop fusion | flops 2949120 | bytes 3932160 | tf_op jit(solution)/shard_map/stack | solution.py:26
  79.7 3.7 %gather_fusion = bf16[4,192,1280]{2,1,0:T(8,128)(2,1)} fusion(bf16[4,192,1280]{2,1,0:T(8,128)(2,1)} %pad_maximum_fusion, s32[1024]{0:T(1024)} %pad_clamp_fusion), kind=kCustom, calls=%fused_computation | custom fusion | bytes 3932176 | tf_op jit(solution)/shard_map/gather | solution.py:28
  83.4 5.0 %convolution_add_fusion = f32[640,1280]{1,0:T(8,128)} fusion(bf16[640,768]{1,0:T(8,128)(2,1)} %bitcast.27, bf16[768,1280]{1,0:T(8,128)(2,1)} %bitcast.25, f32[1280]{0:T(1024)S(1)} %copy-done.87), kind=kOutput, calls=%fused_computation.100 | convolution fusion | flops 1259110400 | bytes 6231040 | tf_op jit(solution)/shard_map/dot_general | solution.py:107
  88.5 5.7 %fusion.5 = bf16[640,1280]{1,0:T(8,128)(2,1)S(1)} fusion(f32[640,1280]{1,0:T(8,128)} %convolution_add_fusion, bf16[640,768]{1,0:T(8,128)(2,1)} %bitcast.29, bf16[768,1280]{1,0:T(8,128)(2,1)} %all-gather.2.cloned.1.call-done), kind=kOutput, calls=%fused_computation.109 | convolution fusion | flops 1273856000 | bytes 7864320 | tf_op jit(solution)/shard_map/dot_general | solution.py:109
  94.1 1.2 copy-done.88
  95.3 2.4 convolution_convert_fusion.2
  98.0 5.4 %convolution_convert_fusion = bf16[768,1280]{1,0:T(8,128)(2,1)} fusion(bf16[640,768]{1,0:T(8,128)(2,1)} %bitcast.30, f32[640,1280]{1,0:T(8,128)} %convolution_add_fusion), kind=kOutput, calls=%fused_computation.101 | convolution fusion | flops 1266647040 | bytes 6225920 | tf_op jit(solution)/shard_map/dot_general | solution.py:114
  103.5 4.9 %convolution_convert_fusion.1 = bf16[768,1280]{1,0:T(8,128)(2,1)} fusion(bf16[640,768]{1,0:T(8,128)(2,1)} %bitcast.28, bf16[640,1280]{1,0:T(8,128)(2,1)} %copy-done.88), kind=kOutput, calls=%fused_computation.102 | convolution fusion | flops 1259274240 | bytes 4587520 | tf_op jit(solution)/shard_map/dot_general | solution.py:117
  108.5 8.0 %all-reduce.6.cloned.1.call-done = bf16[640,768]{1,0:T(8,128)(2,1)} async-done(((bf16[640,768]{1,0:T(8,128)(2,1)}), bf16[640,768]{1,0:T(8,128)(2,1)}) %all-reduce.6.cloned.1.call-update) | async-done | bytes 983056 | tf_op jit(solution)/shard_map/psum | solution.py:132
  116.5 1.5 multiply_reduce_fusion.1
  118.1 1.8 multiply_reduce_fusion
  120.3 1.9 subtract_divide_fusion
  122.2 39.4 %reduce-scatter.5.cloned.1.call-done = bf16[192,1280]{1,0:T(8,128)(2,1)} async-done(((bf16[768,1280]{1,0:T(8,128)(2,1)}), bf16[192,1280]{1,0:T(8,128)(2,1)}) %reduce-scatter.5.cloned.1.call-update) | async-done | bytes 491536 | tf_op jit(solution)/shard_map/reduce_scatter | solution.py:124
  161.6 43.0 %reduce-scatter.3.cloned.1.call-done = bf16[192,1280]{1,0:T(8,128)(2,1)} async-done(((bf16[768,1280]{1,0:T(8,128)(2,1)}), bf16[192,1280]{1,0:T(8,128)(2,1)}) %reduce-scatter.3.cloned.1.call-update) | async-done | bytes 491536 | tf_op jit(solution)/shard_map/reduce_scatter | solution.py:121
  205.0 39.8 %fusion.200 = bf16[10,8,8,768]{3,2,1,0:T(8,128)(2,1)} fusion(f32[10,8,8,768]{3,2,1,0:T(8,128)} %subtract_divide_fusion, bf16[10,8,8,768]{3,2,1,0:T(8,128)(2,1)S(1)} %copy-done, f32[768]{0:T(1024)S(1)} %copy-done.26, f32[768]{0:T(1024)S(1)} %copy-done.28, f32[768]{0:T(1024)S(1)} %copy-done.32, f32[768]{0:T(1024)S(1)} %copy-done.34, f32[768]{0:T(1024)S(1)} %copy-done.36, ...), kind=kLoop, calls=%fused_computation.312 | loop fusion | flops 50135040 | bytes 4113448 | tf_op jit(solution)/shard_map/convert_element_type | solution.py:134
  245.0 2.0 convert_element_type.77
  247.0 2.0 convert_element_type.80
  (205 shorter events, 5.5 us)
Async XLA Ops:
  7.2 81.3 %all-gather.2.cloned.1.call-start = ((), (), s32[]{:S(2)}) async-start(), calls=%async_computation.3 | async-start | bytes 2457600 | tf_op jit(solution)/shard_map/all_gather | solution.py:105
  7.2 51.4 %collective-permute-start = (bf16[192,1280]{1,0:T(8,128)(2,1)}, bf16[192,1280]{1,0:T(8,128)(2,1)}, u32[]{:S(2)}, u32[]{:S(2)}) collective-permute-start(bf16[192,1280]{1,0:T(8,128)(2,1)} %param.20), channel_id=1, source_target_pairs={{0,4},{4,8},{8,12},{12,0},{1,5},{5,9},{9,13},{13,1},{2,6},{6,10},{... | collective-permute-start | bytes 1474568 | tf_op jit(solution)/shard_map/ppermute | solution.py:23
  10.3 51.6 %collective-permute-start.2 = (bf16[192,1280]{1,0:T(8,128)(2,1)}, bf16[192,1280]{1,0:T(8,128)(2,1)}, u32[]{:S(2)}, u32[]{:S(2)}) collective-permute-start(bf16[192,1280]{1,0:T(8,128)(2,1)} %param.20), channel_id=1, source_target_pairs={{4,0},{8,4},{12,8},{0,12},{5,1},{9,5},{13,9},{1,13},{6,2},{10,6},{... | collective-permute-start | bytes 1474568 | tf_op jit(solution)/shard_map/ppermute | solution.py:25
  13.9 41.7 %all-to-all-start = ((bf16[4,2,960]{2,1,0:T(2,128)(2,1)}), bf16[4,2,960]{2,1,0:T(2,128)(2,1)}, u32[]{:S(2)}, u32[]{:S(2)}) async-start(bf16[4,2,960]{2,1,0:T(2,128)(2,1)} %reshape.284), calls=%async_computation | async-start | bytes 32768 | tf_op jit(solution)/shard_map/all_to_all | solution.py:94
  17.7 98.8 %all-reduce.6.cloned.1.call-start = ((), (), s32[]{:S(2)}) async-start(), calls=%async_computation.4 | async-start | bytes 1966080 | tf_op jit(solution)/shard_map/psum | solution.py:132
  58.6 18.4 %collective-permute-start.1 = (bf16[192,1280]{1,0:T(8,128)(2,1)}, bf16[192,1280]{1,0:T(8,128)(2,1)S(1)}, u32[]{:S(2)}, u32[]{:S(2)}) collective-permute-start(bf16[192,1280]{1,0:T(8,128)(2,1)} %collective-permute-done), channel_id=1, source_target_pairs={{0,4},{4,8},{8,12},{12,0},{1,5},{5,9},{9,13},{13,1},{2,6},{6,10},{... | collective-permute-start | bytes 1474568 | tf_op jit(solution)/shard_map/ppermute | solution.py:23
  97.8 63.8 %reduce-scatter.5.cloned.1.call-start = ((), (), s32[]{:S(2)}) async-start(), calls=%async_computation.6 | async-start | bytes 2457600 | tf_op jit(solution)/shard_map/reduce_scatter | solution.py:124
  103.5 101.1 %reduce-scatter.3.cloned.1.call-start = ((), (), s32[]{:S(2)}) async-start(), calls=%async_computation.5 | async-start | bytes 2457600 | tf_op jit(solution)/shard_map/reduce_scatter | solution.py:121
  108.4 136.6 %all-reduce.8.cloned.1.call-start = ((), (), s32[]{:S(2)}) async-start(), calls=%async_computation.7 | async-start | bytes 1966080 | tf_op jit(solution)/shard_map/psum | solution.py:129
  119.9 84.7 %copy-start.4 = (f32[10,768]{1,0:T(8,128)S(1)}, f32[10,768]{1,0:T(8,128)}, u32[]{:S(2)}) copy-start(f32[10,768]{1,0:T(8,128)} %copy-done.3) | copy-start | bytes 92164
  119.9 84.7 %copy-start.8 = (f32[768]{0:T(1024)S(1)}, f32[768]{0:T(1024)}, u32[]{:S(2)}) copy-start(f32[768]{0:T(1024)} %copy-done.7) | copy-start | bytes 9220
  119.9 84.7 %copy-start.10 = (f32[768]{0:T(1024)S(1)}, f32[768]{0:T(1024)}, u32[]{:S(2)}) copy-start(f32[768]{0:T(1024)} %copy-done.9) | copy-start | bytes 9220
  119.9 84.7 %copy-start.12 = (f32[768]{0:T(1024)S(1)}, f32[768]{0:T(1024)}, u32[]{:S(2)}) copy-start(f32[768]{0:T(1024)} %copy-done.11) | copy-start | bytes 9220
  119.9 84.7 %copy-start.14 = (f32[768]{0:T(1024)S(1)}, f32[768]{0:T(1024)}, u32[]{:S(2)}) copy-start(f32[768]{0:T(1024)} %copy-done.13) | copy-start | bytes 9220
  119.9 84.7 %copy-start.16 = (f32[768]{0:T(1024)S(1)}, f32[768]{0:T(1024)}, u32[]{:S(2)}) copy-start(f32[768]{0:T(1024)} %copy-done.15) | copy-start | bytes 9220
  119.9 84.7 %copy-start.18 = (f32[768]{0:T(1024)S(1)}, f32[768]{0:T(1024)}, u32[]{:S(2)}) copy-start(f32[768]{0:T(1024)} %copy-done.17) | copy-start | bytes 9220
  119.9 84.7 %copy-start.20 = (f32[768]{0:T(1024)S(1)}, f32[768]{0:T(1024)}, u32[]{:S(2)}) copy-start(f32[768]{0:T(1024)} %copy-done.19) | copy-start | bytes 9220
  119.9 84.7 %copy-start.22 = (f32[768]{0:T(1024)S(1)}, f32[768]{0:T(1024)}, u32[]{:S(2)}) copy-start(f32[768]{0:T(1024)} %copy-done.21) | copy-start | bytes 9220
  120.0 84.7 %copy-start.24 = (f32[768]{0:T(1024)S(1)}, f32[768]{0:T(1024)}, u32[]{:S(2)}) copy-start(f32[768]{0:T(1024)} %copy-done.23) | copy-start | bytes 9220
  120.0 84.7 %copy-start.26 = (f32[768]{0:T(1024)S(1)}, f32[768]{0:T(1024)}, u32[]{:S(2)}) copy-start(f32[768]{0:T(1024)} %copy-done.25) | copy-start | bytes 9220
  120.0 84.7 %copy-start.28 = (f32[768]{0:T(1024)S(1)}, f32[768]{0:T(1024)}, u32[]{:S(2)}) copy-start(f32[768]{0:T(1024)} %copy-done.27) | copy-start | bytes 9220
  120.0 84.7 %copy-start.30 = (f32[768]{0:T(1024)S(1)}, f32[768]{0:T(1024)}, u32[]{:S(2)}) copy-start(f32[768]{0:T(1024)} %copy-done.29) | copy-start | bytes 9220
  120.0 84.7 %copy-start.32 = (f32[768]{0:T(1024)S(1)}, f32[768]{0:T(1024)}, u32[]{:S(2)}) copy-start(f32[768]{0:T(1024)} %copy-done.31) | copy-start | bytes 9220
  120.0 84.7 %copy-start.34 = (f32[768]{0:T(1024)S(1)}, f32[768]{0:T(1024)}, u32[]{:S(2)}) copy-start(f32[768]{0:T(1024)} %copy-done.33) | copy-start | bytes 9220
  120.0 84.7 %copy-start.36 = (f32[768]{0:T(1024)S(1)}, f32[768]{0:T(1024)}, u32[]{:S(2)}) copy-start(f32[768]{0:T(1024)} %copy-done.35) | copy-start | bytes 9220
  120.0 84.7 %copy-start.38 = (f32[768]{0:T(1024)S(1)}, f32[768]{0:T(1024)}, u32[]{:S(2)}) copy-start(f32[768]{0:T(1024)} %copy-done.37) | copy-start | bytes 9220
  120.0 84.7 %copy-start.40 = (f32[768]{0:T(1024)S(1)}, f32[768]{0:T(1024)}, u32[]{:S(2)}) copy-start(f32[768]{0:T(1024)} %copy-done.39) | copy-start | bytes 9220
  120.0 84.7 %copy-start.42 = (f32[768]{0:T(1024)S(1)}, f32[768]{0:T(1024)}, u32[]{:S(2)}) copy-start(f32[768]{0:T(1024)} %copy-done.41) | copy-start | bytes 9220
  120.1 84.7 %copy-start.44 = (f32[768]{0:T(1024)S(1)}, f32[768]{0:T(1024)}, u32[]{:S(2)}) copy-start(f32[768]{0:T(1024)} %copy-done.43) | copy-start | bytes 9220
  120.1 84.7 %copy-start.46 = (f32[768]{0:T(1024)S(1)}, f32[768]{0:T(1024)}, u32[]{:S(2)}) copy-start(f32[768]{0:T(1024)} %copy-done.45) | copy-start | bytes 9220
  120.1 84.7 %copy-start.48 = (f32[768]{0:T(1024)S(1)}, f32[768]{0:T(1024)}, u32[]{:S(2)}) copy-start(f32[768]{0:T(1024)} %copy-done.47) | copy-start | bytes 9220
  120.1 84.7 %copy-start.50 = (f32[768]{0:T(1024)S(1)}, f32[768]{0:T(1024)}, u32[]{:S(2)}) copy-start(f32[768]{0:T(1024)} %copy-done.49) | copy-start | bytes 9220
  (66 other events, 2197.7 us)
Sparse Core Ops, SparseCore 0:
  12.5 57.2 all-gather.1
  97.9 18.5 all-reduce.5
  118.9 42.6 reduce-scatter.4
  163.9 40.6 reduce-scatter.2
  206.9 38.0 all-reduce.7
